TPU v7x, 256 devices: a whole 4x4x8 slice. The times are simulated.
256 devices in a mesh: ia: 4 (over y), ja: 4 (over x), ka: 16 (over z, core).
Axes of the slice: x: 4, y: 4, z: 8, core: 2. Of those that a mesh axis runs over, the one named last changes fastest.
Arguments:
- blocks: bfloat16 [4, 4, 16, 2, 128, 128, 128], P('ia', 'ja', 'ka'), may hold values from -6 to 6
- first_mode_rows: int32 [4, 4, 16, 2], P('ia', 'ja', 'ka'), may hold values from 0 to 15
- second_mode_rows: int32 [4, 4, 16, 2], P('ia', 'ja', 'ka'), may hold values from 0 to 15
- third_mode_rows: int32 [4, 4, 16, 2], P('ia', 'ja', 'ka'), may hold values from 0 to 3
- filled: int32 [4, 4, 16], P('ia', 'ja', 'ka'), may hold values from 1 to 2, as said below
- owner_one: int32 [64], replicated, may hold values from 0 to 63, each once
- owner_two: int32 [64], replicated, may hold values from 0 to 63, each once
- factor_b: float32 [4, 2048, 256], P('ja', ('ia', 'ka'))
- factor_c: float32 [16, 512, 256], P('ka')
Outputs:
- a_new: float32 [4, 2048, 256], P('ia', ('ja', 'ka'))
- b_new: float32 [4, 2048, 256], P('ja', ('ia', 'ka'))
Inputs may be any that keep to these rules, and one draw needn't show every extreme that they name: Number of nonempty slots of a grid cell; at least one cell has all 2 slots filled. Slots at or beyond this count hold data that is not part of the tensor.
All inputs are finite; a program needn't handle non-finite values.
Results may differ from a plain program's by a relative error of at most 0.0039.
The roundings to bfloat16 on the way count: a program that leaves them out, or rounds other values in their place, can miss the bound.
Values may be sent and summed in bfloat16 or wider, within the bound.
A program may use at most 128 MiB of HBM per device.

v0:
```python
import jax
import jax.numpy as jnp
from jax import lax
from jax.sharding import PartitionSpec as P

EPS = 1e-06


def solve_rows(gram, rows):
    lower = jnp.linalg.cholesky(gram)
    return jax.scipy.linalg.cho_solve((lower, True), rows.T).T


def add_rows(accum, start, contrib):
    current = lax.dynamic_slice_in_dim(accum, start, contrib.shape[0], 0)
    return lax.dynamic_update_slice_in_dim(accum, current + contrib, start, 0)


def batched_sum(inner, weights):
    summed = lax.dot_general(
        inner,
        weights.astype(jnp.float32),
        (((1,), (0,)), ((2,), (1,))),
        precision=lax.Precision.HIGHEST,
        preferred_element_type=jnp.float32,
    )
    return summed.T


def to_logical(stored, owner, piece_rows):
    return stored.reshape(-1, piece_rows, stored.shape[1])[owner].reshape(stored.shape)


def to_stored(logical, owner, piece_rows):
    positions = jnp.arange(owner.shape[0], dtype=jnp.int32)
    inverse = jnp.sum(
        jnp.where(owner[None, :] == positions[:, None], positions[None, :], 0), axis=1
    )
    return logical.reshape(-1, piece_rows, logical.shape[1])[inverse].reshape(logical.shape)


def keep_same(value):
    return value


def partial_value(function, slot):

    def applied(value):
        return function(value, slot)

    return applied


def body(
    blocks,
    first_mode_rows,
    second_mode_rows,
    third_mode_rows,
    filled,
    owner_one,
    owner_two,
    factor_b,
    factor_c,
):
    highest = lax.Precision.HIGHEST
    piece_rows = factor_b.shape[1]
    rank_width = factor_b.shape[2]
    block_edge = blocks.shape[-1]
    slot_count = blocks.shape[3]
    total_one = piece_rows * lax.axis_size("ia") * lax.axis_size("ja") * lax.axis_size("ka")
    slab_rows_one = piece_rows * lax.axis_size("ja") * lax.axis_size("ka")
    slab_rows_two = piece_rows * lax.axis_size("ia") * lax.axis_size("ka")
    own_b = factor_b[0]
    own_c = lax.dynamic_slice_in_dim(
        factor_c[0], lax.axis_index(("ia", "ja")) * piece_rows, piece_rows, 0
    )
    local_b = jnp.dot(own_b.T, own_b, precision=highest, preferred_element_type=jnp.float32)
    local_c = jnp.dot(own_c.T, own_c, precision=highest, preferred_element_type=jnp.float32)
    gram_b, gram_c = lax.psum((local_b, local_c), ("ia", "ja", "ka"))
    stored_b = lax.all_gather(factor_b.astype(jnp.bfloat16), ("ia", "ka"), axis=1, tiled=True)[0]
    half_b = to_logical(stored_b, owner_two, piece_rows)
    half_c = factor_c[0].astype(jnp.bfloat16)
    live_count = filled[0, 0, 0]

    def update_one(partial_sum, slot):
        block = blocks[0, 0, 0, slot]
        b_rows = lax.dynamic_slice_in_dim(
            half_b, second_mode_rows[0, 0, 0, slot] * block_edge, block_edge, 0
        )
        c_rows = lax.dynamic_slice_in_dim(
            half_c, third_mode_rows[0, 0, 0, slot] * block_edge, block_edge, 0
        )
        inner = jnp.dot(
            block.reshape(block_edge * block_edge, block_edge),
            c_rows,
            preferred_element_type=jnp.float32,
        )
        inner = inner.reshape(block_edge, block_edge, rank_width)
        contrib = batched_sum(inner, b_rows)
        return add_rows(partial_sum, first_mode_rows[0, 0, 0, slot] * block_edge, contrib)

    partial_one = jnp.zeros((slab_rows_one, rank_width), jnp.float32)
    for slot in range(slot_count):
        partial_one = lax.cond(
            slot < live_count, partial_value(update_one, slot), keep_same, partial_one
        )
    stored_one = to_stored(partial_one, owner_one, piece_rows)
    system_one = gram_b * gram_c
    summed_own = lax.psum_scatter(stored_one, ("ja", "ka"), scatter_dimension=0, tiled=True)
    a_hat = solve_rows(system_one, summed_own)
    squares_a = lax.psum(jnp.sum(a_hat * a_hat, axis=0), ("ia", "ja", "ka"))
    scale_a = jnp.sqrt(squares_a / total_one + EPS)
    a_own = a_hat / scale_a
    local_a = jnp.dot(a_own.T, a_own, precision=highest, preferred_element_type=jnp.float32)
    gram_a = lax.psum(local_a, ("ia", "ja", "ka"))
    stored_a = lax.all_gather(a_own.astype(jnp.bfloat16)[None], ("ja", "ka"), axis=1, tiled=True)[0]
    half_a = to_logical(stored_a, owner_one, piece_rows)

    def update_two(partial_sum, slot):
        block = blocks[0, 0, 0, slot]
        a_rows = lax.dynamic_slice_in_dim(
            half_a, first_mode_rows[0, 0, 0, slot] * block_edge, block_edge, 0
        )
        c_rows = lax.dynamic_slice_in_dim(
            half_c, third_mode_rows[0, 0, 0, slot] * block_edge, block_edge, 0
        )
        inner = lax.dot_general(
            block.reshape(block_edge, block_edge * block_edge),
            a_rows,
            (((0,), (0,)), ((), ())),
            preferred_element_type=jnp.float32,
        )
        inner = inner.reshape(block_edge, block_edge, rank_width)
        contrib = batched_sum(inner, c_rows)
        return add_rows(partial_sum, second_mode_rows[0, 0, 0, slot] * block_edge, contrib)

    partial_two = jnp.zeros((slab_rows_two, rank_width), jnp.float32)
    for slot in range(slot_count):
        partial_two = lax.cond(
            slot < live_count, partial_value(update_two, slot), keep_same, partial_two
        )
    stored_two = to_stored(partial_two, owner_two, piece_rows)
    summed_two = lax.psum_scatter(stored_two, ("ia", "ka"), scatter_dimension=0, tiled=True)
    b_hat = solve_rows(gram_a * gram_c, summed_two)
    squares_b = lax.psum(jnp.sum(b_hat * b_hat, axis=0), ("ia", "ja", "ka"))
    b_own = b_hat / jnp.sqrt(squares_b / total_one + EPS)
    return (a_own[None], b_own[None])


def solution(mesh):
    return jax.shard_map(
        body,
        mesh=mesh,
        in_specs=(
            P("ia", "ja", "ka", None, None, None, None),
            P("ia", "ja", "ka", None),
            P("ia", "ja", "ka", None),
            P("ia", "ja", "ka", None),
            P("ia", "ja", "ka"),
            P(),
            P(),
            P("ja", ("ia", "ka"), None),
            P("ka", None, None),
        ),
        out_specs=(P("ia", ("ja", "ka"), None), P("ja", ("ia", "ka"), None)),
        check_vma=False,
    )
```

profile of v0, /device:TPU:1, one launch (start us, length us, event | category | flops | bytes accessed | tf_op | source)
XLA Modules:
  0.0 827.5 jit_solution(4852424667202017735)
XLA Ops:
  8.0 1.4 convert_element_type.36
  9.5 2.0 fusion.34
  11.5 2.0 fusion.36
  14.9 0.8 select_reduce_fusion.5
  16.4 1.1 convert_bitcast_fusion
  17.5 75.5 %all-gather.4.cloned.1.call-done = bf16[1,2048,256]{2,1,0:T(8,128)(2,1)} async-done(((bf16[1,32,256]{2,1,0:T(8,128)(2,1)}), bf16[1,2048,256]{2,1,0:T(8,128)(2,1)}) %all-gather.4.cloned.1.call-update) | async-done | bytes 1048592 | tf_op jit(solution)/shard_map/all_gather | solution.py:80
  93.0 1.8 gather_fusion
  94.8 23.3 %conditional.4 = (f32[2048,256]{1,0:T(8,128)}) conditional(s32[]{:T(128)} %bitcast.41, () %tuple.54, (s32[1,1,1,2]{3,2,1,0:T(1,128)}, bf16[512,256]{1,0:T(8,128)(2,1)S(1)}, bf16[1,1,1,2,128,128,128]{6,5,4,3,2,1,0:T(8,128)(2,1)}, s32[1,1,1,2]{3,2,1,0:T(1,128)}, bf16[2048,256]{1,0:T(8,128)(2,1)S(1)}, /*index=5*/s32[1,1,1,2]{3,2,1,0:T(1,128)}) %tuple.134), branch_computations={%region_6.0_spmd, %region_7.0_spmd} | conditional | flops 1082130432 | bytes 83099928 | solution.py:104
  95.5 2.8 slice.76
  98.3 2.4 convolution_bitcast_fusion
  100.7 6.7 copy.52
  107.6 8.2 multiply_reduce_fusion
  116.0 1.5 broadcast.140
  118.1 3.6 gather_fusion.1
  122.1 149.6 %all-reduce.7.cloned.1.call-done = (f32[256,256]{0,1:T(8,128)}, f32[256,256]{0,1:T(8,128)}) async-done(((f32[256,256]{0,1:T(8,128)}, f32[256,256]{0,1:T(8,128)}), (f32[256,256]{0,1:T(8,128)}, f32[256,256]{0,1:T(8,128)})) %all-reduce.7.cloned.1.call-update) | async-done | bytes 524304 | tf_op jit(solution)/shard_map/psum | solution.py:79
  271.6 1.1 mul.94
  272.9 11.7 %cholesky.130 = f32[128,128]{1,0:T(8,128)S(1)} custom-call(f32[128,128]{1,0:T(8,128)S(1)} %cholesky.194), custom_call_target="Cholesky" | custom-call | tf_op jit(solution)/shard_map/jit(cholesky)/cholesky | solution.py:10
  284.7 9.8 %custom-call.15 = f32[1,128,128]{1,2,0:T(8,128)S(1)} custom-call(f32[1,128,128]{2,1,0:T(8,128)S(1)} %get-tuple-element.155), custom_call_target="InvertDiagBlocksLowerTriangular" | custom-call | tf_op jit(solution)/shard_map/jit(cholesky)/cholesky | solution.py:10
  295.0 11.7 %cholesky.147 = f32[128,128]{1,0:T(8,128)S(1)} custom-call(f32[128,128]{1,0:T(8,128)S(1)} %convolution_subtract_fusion.1), custom_call_target="Cholesky" | custom-call | tf_op jit(solution)/shard_map/jit(cholesky)/cholesky | solution.py:10
  308.8 14.6 %while.4 = (s32[]{:T(128)}, f32[256,256]{1,0:T(8,128)S(1)}, s32[2,2]{1,0:T(2,128)S(1)}, f32[2,128,128]{2,1,0:T(8,128)S(1)}, s32[]{:T(128)}) while((s32[]{:T(128)}, f32[256,256]{1,0:T(8,128)S(1)}, s32[2,2]{1,0:T(2,128)S(1)}, f32[2,128,128]{2,1,0:T(8,128)S(1)}, s32[]{:T(128)}) %tuple.103), condition=%wide.while_cond, body=%wide.while_body.sunk | while | flops 2 | bytes 131181 | solution.py:11
  320.0 1.4 bitcast_dynamic-update-slice_fusion.6
  322.0 1.4 bitcast_dynamic-update-slice_fusion.6
  323.4 19.7 %custom-call.16 = f32[2,128,128]{1,2,0:T(8,128)S(1)} custom-call(f32[2,128,128]{2,1,0:T(8,128)S(1)} %get-tuple-element.124), custom_call_target="InvertDiagBlocksLowerTriangular" | custom-call | tf_op jit(solution)/shard_map/jit(_cho_solve)/triangular_solve | solution.py:11
  343.1 0.9 fusion.23
  344.0 0.9 convolution_subtract_fusion.5
  345.9 77.9 %psum.37 = f32[256]{0:T(256)S(1)} all-reduce(f32[256]{0:T(256)S(1)} %multiply_reduce_fusion.5), channel_id=1, replica_groups=mesh['ia'=4,'ja'=4,'ka'=16] {'ia','ja','ka'}, use_global_device_ids=true, to_apply=%region_13.16 | all-reduce | flops 256 | bytes 2048 | tf_op jit(solution)/shard_map/psum | solution.py:111
  424.6 1.1 fusion.46
  425.8 71.7 %all-gather.6.cloned.1.call-done = bf16[2048,256]{1,0:T(8,128)(2,1)} async-done(((bf16[32,256]{1,0:T(8,128)(2,1)}), bf16[2048,256]{1,0:T(8,128)(2,1)}) %all-gather.6.cloned.1.call-update) | async-done | bytes 1048592 | tf_op jit(solution)/shard_map/all_gather | solution.py:116
  497.5 1.8 gather_fusion.2
  499.4 23.6 %conditional.6 = (f32[2048,256]{1,0:T(8,128)}) conditional(s32[]{:T(128)} %bitcast.41, () %tuple.57, (s32[1,1,1,2]{3,2,1,0:T(1,128)S(1)}, bf16[2048,256]{1,0:T(8,128)(2,1)S(1)}, bf16[1,1,1,2,128,128,128]{6,5,4,3,2,1,0:T(8,128)(2,1)}, s32[1,1,1,2]{3,2,1,0:T(1,128)S(1)}, bf16[512,256]{1,0:T(8,128)(2,1)S(1)}, ...), branch_computations={%region_15.18_spmd, %region_16.19_spmd} | conditional | flops 1082130432 | bytes 83099800 | solution.py:139
  499.4 2.5 slice.84
  501.9 3.6 convolution_bitcast_fusion.2
  505.5 6.7 copy.55
  512.4 8.3 multiply_reduce_fusion.2
  520.8 1.5 broadcast.142
  523.1 3.7 gather_fusion.3
  526.8 150.8 %all-reduce.5.cloned.1.call-done = f32[256,256]{0,1:T(8,128)} async-done(((f32[256,256]{0,1:T(8,128)}), f32[256,256]{0,1:T(8,128)}) %all-reduce.5.cloned.1.call-update) | async-done | bytes 262160 | tf_op jit(solution)/shard_map/psum | solution.py:115
  677.6 1.0 mul.96
  678.8 11.7 %cholesky.164 = f32[128,128]{1,0:T(8,128)S(1)} custom-call(f32[128,128]{1,0:T(8,128)S(1)} %cholesky.197), custom_call_target="Cholesky" | custom-call | tf_op jit(solution)/shard_map/jit(cholesky)/cholesky | solution.py:10
  690.6 9.8 %custom-call.17 = f32[1,128,128]{1,2,0:T(8,128)S(1)} custom-call(f32[1,128,128]{2,1,0:T(8,128)S(1)} %get-tuple-element.151), custom_call_target="InvertDiagBlocksLowerTriangular" | custom-call | tf_op jit(solution)/shard_map/jit(cholesky)/cholesky | solution.py:10
  700.9 11.7 %cholesky.181 = f32[128,128]{1,0:T(8,128)S(1)} custom-call(f32[128,128]{1,0:T(8,128)S(1)} %convolution_subtract_fusion), custom_call_target="Cholesky" | custom-call | tf_op jit(solution)/shard_map/jit(cholesky)/cholesky | solution.py:10
  715.2 4.2 while.5
  716.1 1.4 bitcast_dynamic-update-slice_fusion.7
  718.1 1.4 bitcast_dynamic-update-slice_fusion.7
  719.4 19.7 %custom-call.18 = f32[2,128,128]{1,2,0:T(8,128)S(1)} custom-call(f32[2,128,128]{2,1,0:T(8,128)S(1)} %get-tuple-element.125), custom_call_target="InvertDiagBlocksLowerTriangular" | custom-call | tf_op jit(solution)/shard_map/jit(_cho_solve)/triangular_solve | solution.py:11
  739.2 0.9 fusion.27
  740.0 0.9 convolution_subtract_fusion.3
  742.0 77.3 %psum.39 = f32[256]{0:T(256)S(1)} all-reduce(f32[256]{0:T(256)S(1)} %multiply_reduce_fusion.4), channel_id=1, replica_groups=mesh['ia'=4,'ja'=4,'ka'=16] {'ia','ja','ka'}, use_global_device_ids=true, to_apply=%region_22.25 | all-reduce | flops 256 | bytes 2048 | tf_op jit(solution)/shard_map/psum | solution.py:145
  (93 shorter events, 13.1 us)
Async XLA Ops:
  8.0 85.0 %all-gather.4.cloned.1.call-start = ((), (), s32[]{:S(2)}) async-start(), calls=%async_computation.2 | async-start | bytes 1064960 | tf_op jit(solution)/shard_map/all_gather | solution.py:80
  9.4 262.2 %all-reduce.7.cloned.1.call-start = ((), (), s32[]{:S(2)}) async-start(), calls=%async_computation.7 | async-start | bytes 1048576 | tf_op jit(solution)/shard_map/psum | solution.py:79
  13.5 329.6 %reduce-scatter.3.cloned.1.call-start = ((), (), s32[]{:S(2)}) async-start(), calls=%async_computation.3 | async-start | bytes 2129920 | tf_op jit(solution)/shard_map/reduce_scatter | solution.py:109
  100.7 6.7 copy-start.4
  107.5 8.4 %copy-start.7 = (s32[1,1,1,2]{3,2,1,0:T(1,128)S(1)}, s32[1,1,1,2]{3,2,1,0:T(1,128)}, u32[]{:S(2)}) copy-start(s32[1,1,1,2]{3,2,1,0:T(1,128)} %get-tuple-element.85) | copy-start | bytes 28 | tf_op jit(solution)/shard_map/cond
  121.7 302.8 %copy-start.1 = (s32[64]{0:T(128)S(1)}, s32[64]{0:T(128)}, u32[]{:S(2)}) copy-start(s32[64]{0:T(128)} %param.25) | copy-start | bytes 772
  121.8 375.7 %all-gather.6.cloned.1.call-start = ((), (), s32[]{:S(2)}) async-start(), calls=%async_computation.6 | async-start | bytes 1064960 | tf_op jit(solution)/shard_map/all_gather | solution.py:116
  271.6 227.7 %copy-start.2 = (s32[1,1,1,2]{3,2,1,0:T(1,128)S(1)}, s32[1,1,1,2]{3,2,1,0:T(1,128)}, u32[]{:S(2)}) copy-start(s32[1,1,1,2]{3,2,1,0:T(1,128)} %param.23) | copy-start | bytes 28
  271.6 227.7 %copy-start.3 = (s32[1,1,1,2]{3,2,1,0:T(1,128)S(1)}, s32[1,1,1,2]{3,2,1,0:T(1,128)}, u32[]{:S(2)}) copy-start(s32[1,1,1,2]{3,2,1,0:T(1,128)} %param.22) | copy-start | bytes 28
  271.6 227.7 %copy-start.6 = (s32[1,1,1,2]{3,2,1,0:T(1,128)S(1)}, s32[1,1,1,2]{3,2,1,0:T(1,128)}, u32[]{:S(2)}) copy-start(s32[1,1,1,2]{3,2,1,0:T(1,128)} %param.21) | copy-start | bytes 28
  424.5 253.1 %all-reduce.5.cloned.1.call-start = ((), (), s32[]{:S(2)}) async-start(), calls=%async_computation.4 | async-start | bytes 524288 | tf_op jit(solution)/shard_map/psum | solution.py:115
  425.8 313.4 %reduce-scatter.5.cloned.1.call-start = ((), (), s32[]{:S(2)}) async-start(), calls=%async_computation.5 | async-start | bytes 2129920 | tf_op jit(solution)/shard_map/reduce_scatter | solution.py:143
  523.1 154.5 %copy-start = (f32[256,256]{0,1:T(8,128)S(1)}, f32[256,256]{0,1:T(8,128)}, u32[]{:S(2)}) copy-start(f32[256,256]{0,1:T(8,128)} %get-tuple-element.143) | copy-start | bytes 786436
Sparse Core Ops, SparseCore 0:
  12.2 80.7 all-gather.3
  121.9 159.1 reduce-scatter.2
  424.6 72.8 all-gather.5
  527.0 159.5 reduce-scatter.4
Sparse Core Ops, SparseCore 1:
  15.6 256.0 all-reduce.6
  431.3 246.2 all-reduce.4
where the time goes:
time: 837 us; the launch traced here: 827 us
  waiting for transfers between devices  448 us (54%)
  blocking collectives  155 us (19%)
  other arithmetic  133 us (16%)
  local copies, waits for them, and re-layouts  42.5 us (5%)
  between operations  19.3 us (2%)
  matrix products  17.4 us (2%)
  loops' own time  12.2 us (1%)
    psum x1, waiting for transfers between devices, body(): gram_a = lax.psum(local_a, ('ia', 'ja', 'ka'))  151 us
    psum x1, waiting for transfers between devices, body(): gram_b, gram_c = lax.psum((local_b, local_c), ('ia', 'ja', 'ka'))  150 us
    psum x1, blocking collectives, body(): squares_a = lax.psum(jnp.sum(a_hat * a_hat, axis=0), ('ia', 'ja', 'ka'))  77.9 us
    psum x1, blocking collectives, body(): squares_b = lax.psum(jnp.sum(b_hat * b_hat, axis=0), ('ia', 'ja', 'ka'))  77.3 us
    all_gather x1, waiting for transfers between devices, body(): lax.all_gather(factor_b.astype(jnp.bfloat16), ('ia', 'ka'), axis=1, tiled...  75.5 us
    all_gather x1, waiting for transfers between devices, body(): lax.all_gather(a_own.astype(jnp.bfloat16)[None], ('ja', 'ka'), axis=1, ti...  71.7 us
    another operation x13, other arithmetic, solve_rows(): lower = jnp.linalg.cholesky(gram)  68.6 us
    another operation x5, other arithmetic, solve_rows(): return jax.scipy.linalg.cho_solve((lower, True), rows.T).T  39.4 us
  transfers between devices with their start and end apart: 6, of which 4 were waited for; matrix products, arithmetic and copies ran while one was open for 22% of the time, Pallas kernels for 0%

commit v1 on v0

--- a/solution.py
+++ b/solution.py
@@ -4,6 +4,13 @@
 from jax.sharding import PartitionSpec as P
 
 EPS = 1e-06
+
+
+def gather_over(x, mesh_axis, d):
+    size = lax.axis_size(mesh_axis)
+    shards = jnp.stack([x for _ in range(size)])
+    shards = lax.all_to_all(shards, mesh_axis, split_axis=0, concat_axis=0)
+    return jnp.concatenate(shards, axis=d)
 
 
 def solve_rows(gram, rows):
@@ -77,7 +84,7 @@
     local_b = jnp.dot(own_b.T, own_b, precision=highest, preferred_element_type=jnp.float32)
     local_c = jnp.dot(own_c.T, own_c, precision=highest, preferred_element_type=jnp.float32)
     gram_b, gram_c = lax.psum((local_b, local_c), ("ia", "ja", "ka"))
-    stored_b = lax.all_gather(factor_b.astype(jnp.bfloat16), ("ia", "ka"), axis=1, tiled=True)[0]
+    stored_b = gather_over(factor_b.astype(jnp.bfloat16), ("ia", "ka"), 1)[0]
     half_b = to_logical(stored_b, owner_two, piece_rows)
     half_c = factor_c[0].astype(jnp.bfloat16)
     live_count = filled[0, 0, 0]

time: 837 us -> 931 us (1.11)
  waiting for transfers between devices: 448 us -> 531 us
  starting transfers between devices: 0.51 us -> 13.4 us
    reduce_scatter x1, waiting for transfers between devices: 0.02 us -> 79.3 us  [body(): lax.psum_scatter(stored_two, ('ia', 'ka'), scatter_dimension=0, tiled=True)]
    all_gather x1 -> x0, waiting for transfers between devices: 75.5 us -> none  [body(): lax.all_gather(factor_b.astype(jnp.bfloat16), ('ia', 'ka'), axis=1, tiled...]
    psum x1, waiting for transfers between devices: 150 us -> 206 us  [body(): gram_b, gram_c = lax.psum((local_b, local_c), ('ia', 'ja', 'ka'))]
    all_to_all x0 -> x1, waiting for transfers between devices: none -> 23.7 us  [gather_over(): shards = lax.all_to_all(shards, mesh_axis, split_axis=0, concat_axis=0)]
    all_to_all x0 -> x1, starting transfers between devices: none -> 13.2 us  [gather_over(): shards = lax.all_to_all(shards, mesh_axis, split_axis=0, concat_axis=0)]
  transfers between devices with their start and end apart: 6 -> 6, of which waited for: 4 -> 5; matrix products, arithmetic and copies ran while one was open for 22% -> 20% of each run, Pallas kernels for 0% -> 0%
where the time goes in v1:
time: 931 us; the launch traced here: 922 us
  waiting for transfers between devices  531 us (57%)
  blocking collectives  157 us (17%)
  other arithmetic  129 us (14%)
  local copies, waits for them, and re-layouts  42.4 us (5%)
  between operations  19.4 us (2%)
  matrix products  17.4 us (2%)
  starting transfers between devices  13.4 us (1%)
  loops' own time  11.7 us (1%)
    psum x1, waiting for transfers between devices, body(): gram_b, gram_c = lax.psum((local_b, local_c), ('ia', 'ja', 'ka'))  206 us
    psum x1, waiting for transfers between devices, body(): gram_a = lax.psum(local_a, ('ia', 'ja', 'ka'))  151 us
    psum x1, blocking collectives, body(): squares_b = lax.psum(jnp.sum(b_hat * b_hat, axis=0), ('ia', 'ja', 'ka'))  79.5 us
    reduce_scatter x1, waiting for transfers between devices, body(): lax.psum_scatter(stored_two, ('ia', 'ka'), scatter_dimension=0, tiled=True)  79.3 us
    psum x1, blocking collectives, body(): squares_a = lax.psum(jnp.sum(a_hat * a_hat, axis=0), ('ia', 'ja', 'ka'))  77.6 us
    all_gather x1, waiting for transfers between devices, body(): lax.all_gather(a_own.astype(jnp.bfloat16)[None], ('ja', 'ka'), axis=1, ti...  71.8 us
    another operation x13, other arithmetic, solve_rows(): lower = jnp.linalg.cholesky(gram)  68.6 us
    another operation x5, other arithmetic, solve_rows(): return jax.scipy.linalg.cho_solve((lower, True), rows.T).T  39.4 us
  transfers between devices with their start and end apart: 6, of which 5 were waited for; matrix products, arithmetic and copies ran while one was open for 20% of the time, Pallas kernels for 0%

profile of v1, /device:TPU:1, one launch (start us, length us, event | category | flops | bytes accessed | tf_op | source)
XLA Modules:
  0.0 921.5 jit_solution(4666668900096133365)
XLA Ops:
  8.1 0.8 convert_bitcast_fusion.1
  8.9 1.1 stack.2
  10.0 13.2 %all-to-all-start = ((bf16[64,1,32,256]{3,2,1,0:T(8,128)(2,1)}), bf16[64,1,32,256]{3,2,1,0:T(8,128)(2,1)S(1)}, u32[]{:S(2)}, u32[]{:S(2)}) async-start(bf16[64,1,32,256]{3,2,1,0:T(8,128)(2,1)} %stack.2), calls=%async_computation | async-start | bytes 2097152 | tf_op jit(solution)/shard_map/all_to_all | solution.py:12
  23.2 2.0 fusion.34
  25.2 2.0 fusion.36
  28.2 23.7 %all-to-all-done = bf16[64,1,32,256]{3,2,1,0:T(8,128)(2,1)S(1)} async-done(((bf16[64,1,32,256]{3,2,1,0:T(8,128)(2,1)}), bf16[64,1,32,256]{3,2,1,0:T(8,128)(2,1)S(1)}, u32[]{:S(2)}, u32[]{:S(2)}) %all-to-all-start) | async-done | bytes 1048608 | tf_op jit(solution)/shard_map/all_to_all | solution.py:12
  52.5 22.7 %conditional.4 = (f32[2048,256]{1,0:T(8,128)}) conditional(s32[]{:T(128)} %bitcast.41, () %tuple.54, (s32[1,1,1,2]{3,2,1,0:T(1,128)S(1)}, bf16[512,256]{1,0:T(8,128)(2,1)S(1)}, bf16[1,1,1,2,128,128,128]{6,5,4,3,2,1,0:T(8,128)(2,1)}, s32[1,1,1,2]{3,2,1,0:T(1,128)S(1)}, bf16[2048,256]{1,0:T(8,128)(2,1)S(1)}, ...), branch_computations={%region_6.0_spmd, %region_7.0_spmd} | conditional | flops 1082130432 | bytes 83099800 | solution.py:111
  52.6 2.8 slice.76
  55.4 2.4 convolution_bitcast_fusion
  57.8 6.7 copy.52
  64.7 8.3 multiply_reduce_fusion
  73.1 1.5 broadcast.143
  75.5 3.6 gather_fusion.1
  79.2 205.6 %all-reduce.7.cloned.1.call-done = (f32[256,256]{0,1:T(8,128)}, f32[256,256]{0,1:T(8,128)}) async-done(((f32[256,256]{0,1:T(8,128)}, f32[256,256]{0,1:T(8,128)}), (f32[256,256]{0,1:T(8,128)}, f32[256,256]{0,1:T(8,128)})) %all-reduce.7.cloned.1.call-update) | async-done | bytes 524304 | tf_op jit(solution)/shard_map/psum | solution.py:86
  284.8 1.1 mul.94
  286.0 11.7 %cholesky.130 = f32[128,128]{1,0:T(8,128)S(1)} custom-call(f32[128,128]{1,0:T(8,128)S(1)} %cholesky.194), custom_call_target="Cholesky" | custom-call | tf_op jit(solution)/shard_map/jit(cholesky)/cholesky | solution.py:17
  297.8 9.8 %custom-call.15 = f32[1,128,128]{1,2,0:T(8,128)S(1)} custom-call(f32[1,128,128]{2,1,0:T(8,128)S(1)} %get-tuple-element.155), custom_call_target="InvertDiagBlocksLowerTriangular" | custom-call | tf_op jit(solution)/shard_map/jit(cholesky)/cholesky | solution.py:17
  308.1 11.7 %cholesky.147 = f32[128,128]{1,0:T(8,128)S(1)} custom-call(f32[128,128]{1,0:T(8,128)S(1)} %convolution_subtract_fusion.1), custom_call_target="Cholesky" | custom-call | tf_op jit(solution)/shard_map/jit(cholesky)/cholesky | solution.py:17
  321.9 14.5 %while.4 = (s32[]{:T(128)}, f32[256,256]{1,0:T(8,128)S(1)}, s32[2,2]{1,0:T(2,128)S(1)}, f32[2,128,128]{2,1,0:T(8,128)S(1)}, s32[]{:T(128)}) while((s32[]{:T(128)}, f32[256,256]{1,0:T(8,128)S(1)}, s32[2,2]{1,0:T(2,128)S(1)}, f32[2,128,128]{2,1,0:T(8,128)S(1)}, s32[]{:T(128)}) %tuple.103), condition=%wide.while_cond, body=%wide.while_body.sunk | while | flops 2 | bytes 131181 | solution.py:18
  333.1 1.4 bitcast_dynamic-update-slice_fusion.6
  335.1 1.4 bitcast_dynamic-update-slice_fusion.6
  336.5 19.7 %custom-call.16 = f32[2,128,128]{1,2,0:T(8,128)S(1)} custom-call(f32[2,128,128]{2,1,0:T(8,128)S(1)} %get-tuple-element.124), custom_call_target="InvertDiagBlocksLowerTriangular" | custom-call | tf_op jit(solution)/shard_map/jit(_cho_solve)/triangular_solve | solution.py:18
  356.2 0.9 fusion.23
  357.1 0.9 convolution_subtract_fusion.5
  359.0 77.6 %psum.37 = f32[256]{0:T(256)S(1)} all-reduce(f32[256]{0:T(256)S(1)} %multiply_reduce_fusion.5), channel_id=1, replica_groups=mesh['ia'=4,'ja'=4,'ka'=16] {'ia','ja','ka'}, use_global_device_ids=true, to_apply=%region_13.16 | all-reduce | flops 256 | bytes 2048 | tf_op jit(solution)/shard_map/psum | solution.py:118
  437.3 1.1 fusion.46
  438.6 71.8 %all-gather.3.cloned.1.call-done = bf16[2048,256]{1,0:T(8,128)(2,1)} async-done(((bf16[32,256]{1,0:T(8,128)(2,1)}), bf16[2048,256]{1,0:T(8,128)(2,1)}) %all-gather.3.cloned.1.call-update) | async-done | bytes 1048592 | tf_op jit(solution)/shard_map/all_gather | solution.py:123
  510.4 1.8 gather_fusion.2
  512.2 23.6 %conditional.6 = (f32[2048,256]{1,0:T(8,128)}) conditional(s32[]{:T(128)} %bitcast.41, () %tuple.57, (s32[1,1,1,2]{3,2,1,0:T(1,128)S(1)}, bf16[2048,256]{1,0:T(8,128)(2,1)S(1)}, bf16[1,1,1,2,128,128,128]{6,5,4,3,2,1,0:T(8,128)(2,1)}, s32[1,1,1,2]{3,2,1,0:T(1,128)S(1)}, bf16[512,256]{1,0:T(8,128)(2,1)S(1)}, ...), branch_computations={%region_15.18_spmd, %region_16.19_spmd} | conditional | flops 1082130432 | bytes 83099800 | solution.py:146
  512.3 2.5 slice.84
  514.8 3.6 convolution_bitcast_fusion.2
  518.4 6.7 copy.55
  525.2 8.3 multiply_reduce_fusion.2
  533.7 1.5 broadcast.145
  536.0 3.7 gather_fusion.3
  539.7 150.5 %all-reduce.5.cloned.1.call-done = f32[256,256]{0,1:T(8,128)} async-done(((f32[256,256]{0,1:T(8,128)}), f32[256,256]{0,1:T(8,128)}) %all-reduce.5.cloned.1.call-update) | async-done | bytes 262160 | tf_op jit(solution)/shard_map/psum | solution.py:122
  690.2 1.0 mul.96
  691.4 11.7 %cholesky.164 = f32[128,128]{1,0:T(8,128)S(1)} custom-call(f32[128,128]{1,0:T(8,128)S(1)} %cholesky.197), custom_call_target="Cholesky" | custom-call | tf_op jit(solution)/shard_map/jit(cholesky)/cholesky | solution.py:17
  703.2 9.8 %custom-call.17 = f32[1,128,128]{1,2,0:T(8,128)S(1)} custom-call(f32[1,128,128]{2,1,0:T(8,128)S(1)} %get-tuple-element.151), custom_call_target="InvertDiagBlocksLowerTriangular" | custom-call | tf_op jit(solution)/shard_map/jit(cholesky)/cholesky | solution.py:17
  713.5 11.7 %cholesky.181 = f32[128,128]{1,0:T(8,128)S(1)} custom-call(f32[128,128]{1,0:T(8,128)S(1)} %convolution_subtract_fusion), custom_call_target="Cholesky" | custom-call | tf_op jit(solution)/shard_map/jit(cholesky)/cholesky | solution.py:17
  727.8 4.2 while.5
  728.7 1.4 bitcast_dynamic-update-slice_fusion.7
  730.7 1.4 bitcast_dynamic-update-slice_fusion.7
  732.0 19.7 %custom-call.18 = f32[2,128,128]{1,2,0:T(8,128)S(1)} custom-call(f32[2,128,128]{2,1,0:T(8,128)S(1)} %get-tuple-element.125), custom_call_target="InvertDiagBlocksLowerTriangular" | custom-call | tf_op jit(solution)/shard_map/jit(_cho_solve)/triangular_solve | solution.py:18
  751.7 79.3 %reduce-scatter.5.cloned.1.call-done = f32[32,256]{1,0:T(8,128)} async-done(((f32[2048,256]{1,0:T(8,128)}), f32[32,256]{1,0:T(8,128)}) %reduce-scatter.5.cloned.1.call-update) | async-done | bytes 32784 | tf_op jit(solution)/shard_map/reduce_scatter | solution.py:150
  831.0 0.9 fusion.27
  831.9 0.9 convolution_subtract_fusion.3
  833.8 79.5 %psum.39 = f32[256]{0:T(256)S(1)} all-reduce(f32[256]{0:T(256)S(1)} %multiply_reduce_fusion.4), channel_id=1, replica_groups=mesh['ia'=4,'ja'=4,'ka'=16] {'ia','ja','ka'}, use_global_device_ids=true, to_apply=%region_22.25 | all-reduce | flops 256 | bytes 2048 | tf_op jit(solution)/shard_map/psum | solution.py:152
  (93 shorter events, 12.5 us)
Async XLA Ops:
  8.0 20.2 %copy-start.1 = (f32[1,512,256]{2,1,0:T(8,128)S(1)}, f32[1,512,256]{2,1,0:T(8,128)}, u32[]{:S(2)}) copy-start(f32[1,512,256]{2,1,0:T(8,128)} %param.28) | copy-start | bytes 1572868
  8.0 19.2 %copy-start.2 = (s32[64]{0:T(128)S(1)}, s32[64]{0:T(128)}, u32[]{:S(2)}) copy-start(s32[64]{0:T(128)} %param.26) | copy-start | bytes 772
  8.0 19.4 %copy-start.3 = (s32[64]{0:T(128)S(1)}, s32[64]{0:T(128)}, u32[]{:S(2)}) copy-start(s32[64]{0:T(128)} %param.25) | copy-start | bytes 772
  8.0 44.5 %copy-start.6 = (s32[1,1,1,2]{3,2,1,0:T(1,128)S(1)}, s32[1,1,1,2]{3,2,1,0:T(1,128)}, u32[]{:S(2)}) copy-start(s32[1,1,1,2]{3,2,1,0:T(1,128)} %param.21) | copy-start | bytes 28
  8.0 44.5 %copy-start.5 = (s32[1,1,1,2]{3,2,1,0:T(1,128)S(1)}, s32[1,1,1,2]{3,2,1,0:T(1,128)}, u32[]{:S(2)}) copy-start(s32[1,1,1,2]{3,2,1,0:T(1,128)} %param.22) | copy-start | bytes 28
  8.1 44.5 %copy-start.4 = (s32[1,1,1,2]{3,2,1,0:T(1,128)S(1)}, s32[1,1,1,2]{3,2,1,0:T(1,128)}, u32[]{:S(2)}) copy-start(s32[1,1,1,2]{3,2,1,0:T(1,128)} %param.23) | copy-start | bytes 28
  10.0 41.9 %all-to-all-start = ((bf16[64,1,32,256]{3,2,1,0:T(8,128)(2,1)}), bf16[64,1,32,256]{3,2,1,0:T(8,128)(2,1)S(1)}, u32[]{:S(2)}, u32[]{:S(2)}) async-start(bf16[64,1,32,256]{3,2,1,0:T(8,128)(2,1)} %stack.2), calls=%async_computation | async-start | bytes 2097152 | tf_op jit(solution)/shard_map/all_to_all | solution.py:12
  23.2 261.6 %all-reduce.7.cloned.1.call-start = ((), (), s32[]{:S(2)}) async-start(), calls=%async_computation.7 | async-start | bytes 1048576 | tf_op jit(solution)/shard_map/psum | solution.py:86
  27.2 329.0 %reduce-scatter.3.cloned.1.call-start = ((), (), s32[]{:S(2)}) async-start(), calls=%async_computation.3 | async-start | bytes 2129920 | tf_op jit(solution)/shard_map/reduce_scatter | solution.py:116
  79.1 431.3 %all-gather.3.cloned.1.call-start = ((), (), s32[]{:S(2)}) async-start(), calls=%async_computation.6 | async-start | bytes 1064960 | tf_op jit(solution)/shard_map/all_gather | solution.py:123
  437.3 253.0 %all-reduce.5.cloned.1.call-start = ((), (), s32[]{:S(2)}) async-start(), calls=%async_computation.4 | async-start | bytes 524288 | tf_op jit(solution)/shard_map/psum | solution.py:122
  438.5 392.5 %reduce-scatter.5.cloned.1.call-start = ((), (), s32[]{:S(2)}) async-start(), calls=%async_computation.5 | async-start | bytes 2129920 | tf_op jit(solution)/shard_map/reduce_scatter | solution.py:150
  536.0 154.2 %copy-start = (f32[256,256]{0,1:T(8,128)S(1)}, f32[256,256]{0,1:T(8,128)}, u32[]{:S(2)}) copy-start(f32[256,256]{0,1:T(8,128)} %get-tuple-element.143) | copy-start | bytes 786436
Sparse Core Ops, SparseCore 0:
  29.6 255.1 all-reduce.6
  444.5 245.7 all-reduce.4
  694.8 136.1 reduce-scatter.4
Sparse Core Ops, SparseCore 1:
  79.2 158.1 reduce-scatter.2
  437.3 73.0 all-gather.2
